TPU v7x, 32 devices: a whole 2x2x4 slice. The times are simulated.
32 devices in a mesh: groups: 2 (over y), blk: 4 (over z), leaf: 2 (over x), sample: 2 (over core).
Axes of the slice: x: 2, y: 2, z: 4, core: 2. Of those that a mesh axis runs over, the one named last changes fastest.
Arguments:
- residual: float32 [256, 128, 256], P(('groups', 'blk', 'leaf'), 'sample'), parts along dimension 0, may hold values from -60 to 60
- direction: bfloat16 [256, 128, 256], P(('groups', 'blk', 'leaf'), 'sample'), parts along dimension 0, may hold values from -60 to 60
- step: float32 [256], P(('groups', 'sample')), parts along dimension 0, may hold values from 0.2 to 0.8
- coords: bfloat16 [256, 3, 256], P(('groups', 'blk', 'leaf')), parts along dimension 0, may hold values from 0 to 1
- order: int32 [256, 256], P(('groups', 'blk', 'leaf')), parts along dimension 0, may hold values from 0 to 255, each once within a row
- basis: bfloat16 [256, 64, 256], P(('groups', 'blk', 'leaf')), parts along dimension 0, may hold values from -0.5 to 0.5
- leaf_transfer: bfloat16 [256, 64, 64], P(('groups', 'blk', 'leaf')), parts along dimension 0, may hold values from -0.75 to 0.75
- node_transfer: bfloat16 [16, 64, 64], P(('groups', 'blk', 'leaf')), parts along dimension 0, may hold values from -0.75 to 0.75
- near_list: int32 [256, 12], P(('groups', 'blk', 'leaf')), parts along dimension 0, may hold values from 0 to 127, as said below
- coupling_list: int32 [256, 8], P(('groups', 'blk', 'leaf')), parts along dimension 0, may hold values from 0 to 127, as said below
- coupling: bfloat16 [256, 8, 64, 64], P(('groups', 'blk', 'leaf')), parts along dimension 0, may hold values from -0.25 to 0.25
- top_list: int32 [8, 4], P(('groups', 'blk')), parts along dimension 0, may hold values from 0 to 3, as said below
- top_coupling: bfloat16 [8, 4, 64, 64], P(('groups', 'blk')), parts along dimension 0, may hold values from -0.0625 to 0.0625
Outputs:
- residual_next: float32 [256, 128, 256], P(('groups', 'blk', 'leaf'), 'sample'), parts along dimension 0
- direction_next: bfloat16 [256, 128, 256], P(('groups', 'blk', 'leaf'), 'sample'), parts along dimension 0
There are 2 independent parts, one for each index of `groups`. A program takes and returns all parts, laid end to end along the dimension named above; each array names one. Nothing has to cross between parts.
Inputs may be any that keep to these rules, and one draw needn't show every extreme that they name: `near_list`: entry 0 of leaf g is g itself; the other entries are distinct leaves other than g, each at most 16 positions from g around the cycle of 128 leaves; some leaf names both g - 16 and g + 16 (mod 128). `coupling_list`: the entries of leaf g are distinct leaves of the aligned blocks of 16 leaves just before and just after g's own block, around the cycle of 128 leaves, each more than 16 positions from g. `top_list`: the entries of top cluster b name clusters other than b; they may repeat.
All inputs are finite; a program needn't handle non-finite values.
Results may differ from a plain program's by a relative error of at most 0.0065.
Values may be sent and summed in bfloat16 or wider, within the bound.
No kernel may reach another device: no remote copies, remote signals or barrier semaphores. Data moves between devices by JAX's collectives and lax.ppermute only.
A program may use at most 64 MiB of HBM per device.

v0:
```python
import math
import jax
import jax.numpy as jnp
from jax import lax
from jax.sharding import PartitionSpec as P

LEAF_DEV = 16
ROOT_THREE = math.sqrt(3.0)
LENGTH = 0.3
AMPLITUDE = 0.25
NUGGET = 0.5


def padded(array, sides, width):
    for axis, dim in sides:
        count, length = (lax.axis_size(axis), array.shape[dim])
        up = [(i, (i + 1) % count) for i in range(count)]
        down = [(j, i) for i, j in up]
        last = lax.slice_in_dim(array, length - width, length, axis=dim)
        initial = lax.slice_in_dim(array, 0, width, axis=dim)
        before = lax.ppermute(last, axis, up)
        after = lax.ppermute(initial, axis, down)
        array = jnp.concatenate([before, array, after], axis=dim)
    return array


def swapped(array, axis, bit):
    return lax.ppermute(array, axis, [(i, i ^ 1 << bit) for i in range(lax.axis_size(axis))])


def matern(own_offsets, near_offsets, gap_leaves, spread):
    gap_x = (
        own_offsets[0][:, None] - near_offsets[0][None, :] + gap_leaves.astype(jnp.float32) * spread
    )
    gap_y = own_offsets[1][:, None] - near_offsets[1][None, :]
    gap_z = own_offsets[2][:, None] - near_offsets[2][None, :]
    scaled = jnp.sqrt(gap_x * gap_x + gap_y * gap_y + gap_z * gap_z) * (ROOT_THREE / LENGTH)
    return AMPLITUDE * (1.0 + scaled) * jnp.exp(-scaled)


def tile_block(own_offsets, near_offsets, gap_leaves, spread):
    inner = jax.vmap(matern, in_axes=(None, 0, 0, None))
    return jax.vmap(inner, in_axes=(0, 0, 0, None))(own_offsets, near_offsets, gap_leaves, spread)


def on_device(
    residual,
    direction,
    step,
    coords,
    order,
    basis,
    leaf_transfer,
    node_transfer,
    near_list,
    coupling_list,
    coupling,
    top_list,
    top_coupling,
):
    leaf_dev = direction.shape[0]
    samples = direction.shape[1]
    points = direction.shape[2]
    blk_count = lax.axis_size("blk")
    leaf_count = lax.axis_size("leaf")
    leaf_total = leaf_dev * blk_count * leaf_count
    device = lax.axis_index("blk") * leaf_count + lax.axis_index("leaf")
    first_leaf = device * leaf_dev
    spread = 0.5 / LEAF_DEV
    old_norm = lax.psum(jnp.sum(residual * residual, axis=(0, 2)), ("blk", "leaf"))
    packed = jnp.concatenate([direction, coords], axis=1)
    widened = padded(packed, ((("blk", "leaf"), 0),), leaf_dev)
    anchor = first_leaf - leaf_dev
    own_offsets_all = coords.astype(jnp.float32)
    slot_ids = jnp.mod(near_list - anchor, leaf_total)
    window_values = widened[:, :samples, :]
    window_offsets = widened[:, samples:, :]
    half_rows = leaf_dev // 2
    side = lax.axis_index("sample")
    partner_values = swapped(window_values, "sample", 0)
    all_columns = jnp.where(
        side == 0,
        jnp.concatenate([window_values, partner_values], axis=1),
        jnp.concatenate([partner_values, window_values], axis=1),
    )
    base = side * half_rows
    blocks = 4
    columns = all_columns.shape[1]

    def near_block(block_index):
        start_at = base + block_index * blocks
        slot_rows = lax.dynamic_slice_in_dim(slot_ids, start_at, blocks, 0)
        name_rows = lax.dynamic_slice_in_dim(near_list, start_at, blocks, 0)
        leaf_ids = first_leaf + start_at + jnp.arange(blocks, dtype=jnp.int32)
        near_values = all_columns[slot_rows]
        near_offsets = window_offsets[slot_rows].astype(jnp.float32)
        own_offsets = lax.dynamic_slice_in_dim(own_offsets_all, start_at, blocks, 0)
        gap_leaves = (
            jnp.mod(leaf_ids[:, None] - name_rows + leaf_total // 2, leaf_total) - leaf_total // 2
        )
        kernel_tiles = tile_block(own_offsets, near_offsets, gap_leaves, spread).astype(
            jnp.bfloat16
        )
        return jnp.einsum(
            "lkab,lksb->lsa", kernel_tiles, near_values, preferred_element_type=jnp.float32
        )

    mapped = lax.map(near_block, jnp.arange(half_rows // blocks, dtype=jnp.int32))
    own_rows = mapped.reshape(half_rows, columns, points)
    kept_part = lax.dynamic_slice_in_dim(own_rows, side * samples, samples, 1)
    given_part = lax.dynamic_slice_in_dim(own_rows, (1 - side) * samples, samples, 1)
    received = swapped(given_part.astype(jnp.bfloat16), "sample", 0).astype(given_part.dtype)
    near_field = jnp.where(
        side == 0,
        jnp.concatenate([kept_part, received], axis=0),
        jnp.concatenate([received, kept_part], axis=0),
    )
    inverse = jnp.argsort(order, axis=1)
    natural_values = jnp.take_along_axis(basis, inverse[:, None, :], axis=2)
    expansion_weights = jnp.einsum(
        "ejt,ekt->ekj", natural_values, direction, preferred_element_type=jnp.float32
    ).astype(jnp.bfloat16)
    node_coef = jnp.einsum(
        "lrk,lsk->sr", leaf_transfer, expansion_weights, preferred_element_type=jnp.float32
    ).astype(jnp.bfloat16)
    lifted = jnp.einsum(
        "rk,sk->sr", node_transfer[0], node_coef, preferred_element_type=jnp.float32
    )
    top_node = lax.psum(lifted, "leaf").astype(jnp.bfloat16)
    every_top = lax.all_gather(top_node[None], "blk", axis=0, tiled=True)
    chosen = every_top[top_list[0]]
    incoming = jnp.einsum(
        "krj,ksj->sr", top_coupling[0], chosen, preferred_element_type=jnp.float32
    )
    incoming = incoming.astype(jnp.bfloat16)
    down_coef = jnp.einsum(
        "rk,sr->sk", node_transfer[0], incoming, preferred_element_type=jnp.float32
    ).astype(jnp.bfloat16)
    coef_wide = padded(expansion_weights, ((("blk", "leaf"), 0),), leaf_dev)
    paired_block = coef_wide[jnp.mod(coupling_list - (first_leaf - leaf_dev), leaf_total)]
    upward_gathered = jnp.einsum(
        "lrk,sr->lsk", leaf_transfer, down_coef, preferred_element_type=jnp.float32
    )
    upward_gathered = upward_gathered + jnp.einsum(
        "ohvd,ohgd->ogv", coupling, paired_block, preferred_element_type=jnp.float32
    )
    upward_gathered = upward_gathered.astype(jnp.bfloat16)
    distant_field = jnp.einsum(
        "bfw,baf->baw", natural_values, upward_gathered, preferred_element_type=jnp.float32
    )
    product_image = NUGGET * direction.astype(jnp.float32) + near_field + distant_field
    residual_next = residual - step[None, :, None] * product_image
    new_square = jnp.sum(residual_next * residual_next, axis=(0, 2))
    new_norm = lax.psum(new_square, ("blk", "leaf"))
    beta_ratio = new_norm / old_norm
    direction_next = (
        residual_next + beta_ratio[None, :, None] * direction.astype(jnp.float32)
    ).astype(jnp.bfloat16)
    return (residual_next, direction_next)


def solution(mesh):
    in_specs = (
        P(("groups", "blk", "leaf"), "sample", None),
        P(("groups", "blk", "leaf"), "sample", None),
        P(("groups", "sample")),
        P(("groups", "blk", "leaf"), None, None),
        P(("groups", "blk", "leaf"), None),
        P(("groups", "blk", "leaf"), None, None),
        P(("groups", "blk", "leaf"), None, None),
        P(("groups", "blk", "leaf"), None, None),
        P(("groups", "blk", "leaf"), None),
        P(("groups", "blk", "leaf"), None),
        P(("groups", "blk", "leaf"), None, None, None),
        P(("groups", "blk"), None),
        P(("groups", "blk"), None, None, None),
    )
    out_specs = (
        P(("groups", "blk", "leaf"), "sample", None),
        P(("groups", "blk", "leaf"), "sample", None),
    )
    return jax.shard_map(
        on_device, mesh=mesh, in_specs=in_specs, out_specs=out_specs, check_vma=False
    )
```

profile of v0, /device:TPU:0, one launch (start us, length us, event | category | flops | bytes accessed | tf_op | source)
XLA Modules:
  0.0 217.3 jit_solution(16189384715876912534)
XLA Ops:
  10.1 2.9 %collective-permute-start = (bf16[16,67,256]{2,0,1:T(8,128)(2,1)S(1)}, bf16[16,67,256]{2,0,1:T(8,128)(2,1)S(1)}, u32[]{:S(2)}, u32[]{:S(2)}) collective-permute-start(bf16[16,67,256]{2,0,1:T(8,128)(2,1)S(1)} %get-tuple-element.173), channel_id=1, source_target_pairs={{0,2},{2,4},{4,6},{6,8},{8,10},{10,12},{12,14},{14,0},{1,3},{3,5},... | collective-permute-start | bytes 1646600 | tf_op jit(solution)/shard_map/ppermute | solution.py:21
  13.1 3.0 %collective-permute-start.1 = (bf16[16,67,256]{2,0,1:T(8,128)(2,1)S(1)}, bf16[16,67,256]{2,0,1:T(8,128)(2,1)}, u32[]{:S(2)}, u32[]{:S(2)}) collective-permute-start(bf16[16,67,256]{2,0,1:T(8,128)(2,1)S(1)} %get-tuple-element.173), channel_id=1, source_target_pairs={{2,0},{4,2},{6,4},{8,6},{10,8},{12,10},{14,12},{0,14},{3,1},{5,3},... | collective-permute-start | bytes 1646600 | tf_op jit(solution)/shard_map/ppermute | solution.py:22
  17.6 1.9 multiply_reduce_fusion
  20.2 16.4 %collective-permute-done = bf16[16,67,256]{2,0,1:T(8,128)(2,1)S(1)} collective-permute-done((bf16[16,67,256]{2,0,1:T(8,128)(2,1)S(1)}, bf16[16,67,256]{2,0,1:T(8,128)(2,1)S(1)}, u32[]{:S(2)}, u32[]{:S(2)}) %collective-permute-start) | collective-permute-done | bytes 548896 | tf_op jit(solution)/shard_map/ppermute | solution.py:21
  36.5 2.3 %collective-permute-done.1 = bf16[16,67,256]{2,0,1:T(8,128)(2,1)} collective-permute-done((bf16[16,67,256]{2,0,1:T(8,128)(2,1)S(1)}, bf16[16,67,256]{2,0,1:T(8,128)(2,1)}, u32[]{:S(2)}, u32[]{:S(2)}) %collective-permute-start.1) | collective-permute-done | bytes 548896 | tf_op jit(solution)/shard_map/ppermute | solution.py:22
  45.4 40.6 %gather_fusion.4 = bf16[4096,64]{1,0:T(8,128)(2,1)} fusion(bf16[16,64,256]{1,2,0:T(8,128)(2,1)S(1)} %copy.38, s32[4096]{0:T(1024)S(1)} %bitcast.104), kind=kCustom, calls=%fused_computation.4 | custom fusion | bytes 1081344 | tf_op jit(solution)/shard_map/jit(take_along_axis)/gather | solution.py:119
  86.0 2.4 %copy.39 = bf16[16,256,64]{1,2,0:T(8,128)(2,1)} copy(bf16[16,256,64]{2,1,0:T(8,128)(2,1)} %bitcast.109) | data formatting | bytes 1048576 | tf_op jit(solution)/shard_map/jit(take_along_axis)/gather | solution.py:119
  88.4 2.2 %fusion.12 = bf16[16,64,64]{1,2,0:T(8,128)(2,1)} fusion(bf16[16,64,256]{2,1,0:T(8,128)(2,1)} %param.16, bf16[16,256,64]{1,2,0:T(8,128)(2,1)} %copy.39, pred[16,256]{1,0:T(8,128)(4,1)S(1)} %compare_and_fusion), kind=kOutput, calls=%fused_computation.37 | convolution fusion | flops 33882112 | bytes 1183744 | tf_op jit(solution)/shard_map/ejt,ekt->ekj/dot_general | solution.py:120
  91.0 4.3 %collective-permute-start.5 = (bf16[16,64,64]{1,2,0:T(8,128)(2,1)}, bf16[16,64,64]{1,2,0:T(8,128)(2,1)}, u32[]{:S(2)}, u32[]{:S(2)}) collective-permute-start(bf16[16,64,64]{1,2,0:T(8,128)(2,1)} %fusion.12), channel_id=1, source_target_pairs={{2,0},{4,2},{6,4},{8,6},{10,8},{12,10},{14,12},{0,14},{3,1},{5,3},... | collective-permute-start | bytes 393224 | tf_op jit(solution)/shard_map/ppermute | solution.py:22
  96.7 11.0 %psum.21 = bf16[64,64]{1,0:T(8,128)(2,1)S(1)} all-reduce(f32[64,64]{1,0:T(8,128)S(1)} %fusion.17), channel_id=1, replica_groups=mesh['groups'=2,'blk'=4,'leaf'=2,'sample'=2] {'leaf'}, use_global_device_ids=true, to_apply=%region_3.4 | all-reduce | flops 4096 | bytes 24576 | tf_op jit(solution)/shard_map/psum | solution.py:129
  107.7 13.5 %all-gather = bf16[256,64]{1,0:T(8,128)(2,1)S(1)} all-gather(bf16[64,64]{1,0:T(8,128)(2,1)S(1)} %psum.21), channel_id=2, replica_groups=mesh['groups'=2,'blk'=4,'leaf'=2,'sample'=2] {'blk'}, dimensions={0}, use_global_device_ids=true | all-gather | bytes 40960 | tf_op jit(solution)/shard_map/all_gather | solution.py:130
  124.5 3.1 %maximum_select_fusion = bf16[48,128,256]{2,0,1:T(8,128)(2,1)S(1)} fusion(bf16[48,64,256]{2,0,1:T(8,128)(2,1)} %collective-permute-done.2, bf16[48,64,256]{2,0,1:T(8,128)(2,1)} %slice.57, pred[]{:T(512)S(6)} %eq.12), kind=kLoop, calls=%fused_computation.28 | loop fusion | flops 4718592 | bytes 6291457 | tf_op jit(solution)/shard_map/jit(_where)/select_n | solution.py:81
  127.7 2.8 %copy.36 = bf16[48,128,256]{2,1,0:T(8,128)(2,1)} copy(bf16[48,128,256]{2,0,1:T(8,128)(2,1)S(1)} %maximum_select_fusion) | data formatting | bytes 6291456 | tf_op jit(solution)/shard_map/while | solution.py:108
  130.4 42.3 %while.12 = (s32[]{:T(128)}, f32[2,4,128,256]{3,2,1,0:T(8,128)}, s32[2]{0:T(128)S(1)}, s32[]{:T(128)}, s32[16,12]{1,0:T(8,128)}, /*index=5*/bf16[48,128,256]{2,1...) while((s32[]{:T(128)}, f32[2,4,128,256]{3,2,1,0:T(8,128)}, ...), condition=%wide.region_1.0_spmd, body=%wide.region_0.0_spmd.sunk | while | flops 852494208 | bytes 11184823 | solution.py:108
  134.2 4.4 %gather_fusion = bf16[48,128,256]{2,1,0:T(8,128)(2,1)} fusion(bf16[48,128,256]{2,1,0:T(8,128)(2,1)} %get-tuple-element.290, s32[1024]{0:T(1024)S(1)} %pad_clamp_fusion.4), kind=kCustom, calls=%fused_computation.clone.1 | custom fusion | bytes 6291648 | tf_op jit(solution)/shard_map/while/body/eval_jaxpr/gather | solution.py:95
  139.4 12.2 %fusion.54 = f32[2,4,128,256]{3,2,1,0:T(8,128)} fusion(f32[2,4,128,256]{3,2,1,0:T(8,128)} %get-tuple-element.270, s32[]{:T(128)} %get-tuple-element.269, bf16[4,12,128,256]{3,2,1,0:T(8,128)(2,1)} %bitcast.105, f32[4,12,256]{2,1,0:T(8,128)S(1)} %copy.62, f32[4,256]{1,0:T(4,128)S(1)} %get-tuple-element.248, f32[4,12,256]{2,1,0:T(8,128)S(1)} %copy.63, ...), kind=kOutput, calls=%fused_computation.8.clone.1 | convolution fusion | flops 852492288 | bytes 3830464 | tf_op jit(solution)/shard_map/while/body/eval_jaxpr/lkab,lksb->lsa/dot_general | solution.py:104
  155.4 4.4 %gather_fusion = bf16[48,128,256]{2,1,0:T(8,128)(2,1)} fusion(bf16[48,128,256]{2,1,0:T(8,128)(2,1)} %get-tuple-element.290, s32[1024]{0:T(1024)S(1)} %pad_clamp_fusion.4), kind=kCustom, calls=%fused_computation.clone.1 | custom fusion | bytes 6291648 | tf_op jit(solution)/shard_map/while/body/eval_jaxpr/gather | solution.py:95
  160.6 12.1 %fusion.54 = f32[2,4,128,256]{3,2,1,0:T(8,128)} fusion(f32[2,4,128,256]{3,2,1,0:T(8,128)} %get-tuple-element.270, s32[]{:T(128)} %get-tuple-element.269, bf16[4,12,128,256]{3,2,1,0:T(8,128)(2,1)} %bitcast.105, f32[4,12,256]{2,1,0:T(8,128)S(1)} %copy.62, f32[4,256]{1,0:T(4,128)S(1)} %get-tuple-element.248, f32[4,12,256]{2,1,0:T(8,128)S(1)} %copy.63, ...), kind=kOutput, calls=%fused_computation.8.clone.1 | convolution fusion | flops 852492288 | bytes 3830464 | tf_op jit(solution)/shard_map/while/body/eval_jaxpr/lkab,lksb->lsa/dot_general | solution.py:104
  172.7 1.8 dynamic-slice_convert_fusion
  176.8 2.1 gather_fusion.3
  179.0 1.9 constant_dynamic-slice_fusion
  181.9 4.6 %multiply_reduce_fusion.1 = (f32[64]{0:T(128)S(1)}, f32[16,64,256]{2,1,0:T(8,128)}) fusion(f32[16,64,256]{2,1,0:T(8,128)} %param.15, bf16[16,256,64]{1,2,0:T(8,128)(2,1)} %copy.39, pred[16,256]{1,0:T(8,128)(4,1)S(1)} %copy-done.12, f32[16,64,64]{2,1,0:T(8,128)} %convolution_bitcast_fusion.1, bf16[16,8,64,64]{2,3,1,0:T(8,128)(2,1)} %bitcast.107, ...), kind=kOutput, calls=%fused_computation.54 | convolution fusion | flops 103940032 | bytes 6558209 | tf_op jit(solution)/shard_map/bfw,baf->baw/dot_general | solution.py:148
  186.5 21.7 %all-reduce = (f32[64]{0:T(128)S(1)}, f32[64]{0:T(128)S(1)}) all-reduce(f32[64]{0:T(128)S(1)} %get-tuple-element.174, f32[64]{0:T(128)S(1)} %copy-done.14), channel_id=1, replica_groups=mesh['groups'=2,'blk'=4,'leaf'=2,'sample'=2] {'blk','leaf'}, use_global_device_ids=true, to_apply=%region_5.6 | all-reduce | flops 128 | bytes 1024 | tf_op jit(solution)/shard_map/psum | solution.py:154
  208.2 2.2 %fusion.23 = bf16[16,64,256]{2,1,0:T(8,128)(2,1)} fusion(f32[16,64,256]{2,1,0:T(8,128)} %get-tuple-element.175, bf16[16,64,256]{2,1,0:T(8,128)(2,1)S(1)} %copy-done.3, f32[64]{0:T(128)S(1)} %div.3), kind=kLoop, calls=%fused_computation.51 | loop fusion | flops 1048576 | bytes 2097408 | tf_op jit(solution)/shard_map/convert_element_type | solution.py:158
  (95 shorter events, 27.5 us)
Async XLA Ops:
  7.2 174.7 %copy-start = (bf16[16,8,64,64]{3,2,1,0:T(8,128)(2,1)S(1)}, bf16[16,8,64,64]{3,2,1,0:T(8,128)(2,1)}, u32[]{:S(2)}) copy-start(bf16[16,8,64,64]{3,2,1,0:T(8,128)(2,1)} %param.25) | copy-start | bytes 3145732
  7.2 37.5 %sort.19.cloned.1.call-start = ((), (), s32[]{:S(2)}) async-start(), calls=%async_computation | async-start | bytes 98336 | tf_op jit(solution)/shard_map/jit(argsort)/sort | solution.py:118
  10.1 31.2 %copy-start.1 = (bf16[16,67,256]{2,0,1:T(8,128)(2,1)}, bf16[16,67,256]{2,0,1:T(8,128)(2,1)S(1)}, u32[]{:S(2)}) copy-start(bf16[16,67,256]{2,0,1:T(8,128)(2,1)S(1)} %get-tuple-element.173) | copy-start | bytes 1646596
  10.1 26.4 %collective-permute-start = (bf16[16,67,256]{2,0,1:T(8,128)(2,1)S(1)}, bf16[16,67,256]{2,0,1:T(8,128)(2,1)S(1)}, u32[]{:S(2)}, u32[]{:S(2)}) collective-permute-start(bf16[16,67,256]{2,0,1:T(8,128)(2,1)S(1)} %get-tuple-element.173), channel_id=1, source_target_pairs={{0,2},{2,4},{4,6},{6,8},{8,10},{10,12},{12,14},{14,0},{1,3},{3,5},... | collective-permute-start | bytes 1646600 | tf_op jit(solution)/shard_map/ppermute | solution.py:21
  13.1 25.8 %collective-permute-start.1 = (bf16[16,67,256]{2,0,1:T(8,128)(2,1)S(1)}, bf16[16,67,256]{2,0,1:T(8,128)(2,1)}, u32[]{:S(2)}, u32[]{:S(2)}) collective-permute-start(bf16[16,67,256]{2,0,1:T(8,128)(2,1)S(1)} %get-tuple-element.173), channel_id=1, source_target_pairs={{2,0},{4,2},{6,4},{8,6},{10,8},{12,10},{14,12},{0,14},{3,1},{5,3},... | collective-permute-start | bytes 1646600 | tf_op jit(solution)/shard_map/ppermute | solution.py:22
  20.2 21.7 %copy-start.9 = (s32[16,12]{1,0:T(8,128)S(1)}, s32[16,12]{1,0:T(8,128)}, u32[]{:S(2)}) copy-start(s32[16,12]{1,0:T(8,128)} %param.23) | copy-start | bytes 2308
  36.5 4.8 %copy-start.4 = (bf16[16,67,256]{2,0,1:T(8,128)(2,1)}, bf16[16,67,256]{2,0,1:T(8,128)(2,1)S(1)}, u32[]{:S(2)}) copy-start(bf16[16,67,256]{2,0,1:T(8,128)(2,1)S(1)} %collective-permute-done) | copy-start | bytes 1646596
  41.3 83.2 %collective-permute-start.2 = (bf16[48,64,256]{2,0,1:T(8,128)(2,1)}, bf16[48,64,256]{2,0,1:T(8,128)(2,1)}, u32[]{:S(2)}, u32[]{:S(2)}) collective-permute-start(bf16[48,64,256]{2,0,1:T(8,128)(2,1)} %slice.57), channel_id=1, source_target_pairs={{0,1},{1,0},{2,3},{3,2},{4,5},{5,4},{6,7},{7,6},{8,9},{9,8},{10,11... | collective-permute-start | bytes 4718600 | tf_op jit(solution)/shard_map/ppermute | solution.py:28
  45.4 43.0 %copy-start.8 = (s32[16,256]{1,0:T(8,128)S(1)}, s32[16,256]{1,0:T(8,128)}, u32[]{:S(2)}) copy-start(s32[16,256]{1,0:T(8,128)} %get-tuple-element.131) | copy-start | bytes 49156
  45.4 50.0 %copy-start.7 = (bf16[1,64,64]{2,1,0:T(8,128)(2,1)S(1)}, bf16[1,64,64]{2,1,0:T(8,128)(2,1)}, u32[]{:S(2)}) copy-start(bf16[1,64,64]{2,1,0:T(8,128)(2,1)} %param.22) | copy-start | bytes 24580
  86.0 9.4 %copy-start.6 = (bf16[16,64,64]{2,1,0:T(8,128)(2,1)S(1)}, bf16[16,64,64]{2,1,0:T(8,128)(2,1)}, u32[]{:S(2)}) copy-start(bf16[16,64,64]{2,1,0:T(8,128)(2,1)} %param.21) | copy-start | bytes 393220
  86.0 37.7 %copy-start.2 = (bf16[16,67,256]{2,0,1:T(8,128)(2,1)S(1)}, bf16[16,67,256]{2,0,1:T(8,128)(2,1)}, u32[]{:S(2)}) copy-start(bf16[16,67,256]{2,0,1:T(8,128)(2,1)} %copy-done.1) | copy-start | bytes 1646596
  86.0 37.7 %copy-start.5 = (bf16[16,67,256]{2,0,1:T(8,128)(2,1)S(1)}, bf16[16,67,256]{2,0,1:T(8,128)(2,1)}, u32[]{:S(2)}) copy-start(bf16[16,67,256]{2,0,1:T(8,128)(2,1)} %copy-done.4) | copy-start | bytes 1646596
  88.4 2.6 %copy-start.11 = (pred[16,256]{1,0:T(8,128)(4,1)}, pred[16,256]{1,0:T(8,128)(4,1)S(1)}, u32[]{:S(2)}) copy-start(pred[16,256]{1,0:T(8,128)(4,1)S(1)} %compare_and_fusion) | copy-start | bytes 12292
  90.6 84.9 %collective-permute-start.4 = (bf16[16,64,64]{1,2,0:T(8,128)(2,1)}, bf16[16,64,64]{1,2,0:T(8,128)(2,1)}, u32[]{:S(2)}, u32[]{:S(2)}) collective-permute-start(bf16[16,64,64]{1,2,0:T(8,128)(2,1)} %fusion.12), channel_id=1, source_target_pairs={{0,2},{2,4},{4,6},{6,8},{8,10},{10,12},{12,14},{14,0},{1,3},{3,5},... | collective-permute-start | bytes 393224 | tf_op jit(solution)/shard_map/ppermute | solution.py:21
  91.0 84.5 %collective-permute-start.5 = (bf16[16,64,64]{1,2,0:T(8,128)(2,1)}, bf16[16,64,64]{1,2,0:T(8,128)(2,1)}, u32[]{:S(2)}, u32[]{:S(2)}) collective-permute-start(bf16[16,64,64]{1,2,0:T(8,128)(2,1)} %fusion.12), channel_id=1, source_target_pairs={{2,0},{4,2},{6,4},{8,6},{10,8},{12,10},{14,12},{0,14},{3,1},{5,3},... | collective-permute-start | bytes 393224 | tf_op jit(solution)/shard_map/ppermute | solution.py:22
  130.4 46.4 %copy-start.10 = (s32[1024]{0:T(1024)S(1)}, s32[1024]{0:T(1024)}, u32[]{:S(2)}) copy-start(s32[1024]{0:T(1024)} %pad_clamp_fusion.1) | copy-start | bytes 12292
  174.5 6.4 %collective-permute-start.3 = (bf16[8,64,256]{2,1,0:T(8,128)(2,1)}, bf16[8,64,256]{2,1,0:T(8,128)(2,1)}, u32[]{:S(2)}, u32[]{:S(2)}) collective-permute-start(bf16[8,64,256]{2,1,0:T(8,128)(2,1)} %dynamic-slice_convert_fusion), channel_id=1, source_target_pairs={{0,1},{1,0},{2,3},{3,2},{4,5},{5,4},{6,7},{7,6},{8,9},{9,8},{10,11... | collective-permute-start | bytes 786440 | tf_op jit(solution)/shard_map/ppermute | solution.py:28
  176.8 5.1 %copy-start.3 = (bf16[16,64,256]{2,1,0:T(8,128)(2,1)S(1)}, bf16[16,64,256]{2,1,0:T(8,128)(2,1)}, u32[]{:S(2)}) copy-start(bf16[16,64,256]{2,1,0:T(8,128)(2,1)} %param.16) | copy-start | bytes 1572868
  176.8 5.1 %copy-start.12 = (pred[16,256]{1,0:T(8,128)(4,1)S(1)}, pred[16,256]{1,0:T(8,128)(4,1)}, u32[]{:S(2)}) copy-start(pred[16,256]{1,0:T(8,128)(4,1)} %copy-done.11) | copy-start | bytes 12292
  176.8 5.1 %copy-start.13 = (f32[64]{0:T(128)S(1)}, f32[64]{0:T(128)}, u32[]{:S(2)}) copy-start(f32[64]{0:T(128)} %param.17) | copy-start | bytes 772
  181.9 4.6 %copy-start.14 = (f32[64]{0:T(128)S(1)}, f32[64]{0:T(128)}, u32[]{:S(2)}) copy-start(f32[64]{0:T(128)} %multiply_reduce_fusion) | copy-start | bytes 772
Sparse Core Ops, SparseCore 0:
  16.9 2.5 sort.21.cloned.1.call-done
  (1 shorter events, 0.0 us)
where the time goes:
time: 218 us; the launch traced here: 217 us
  local copies, waits for them, and re-layouts  71.6 us (33%)
  blocking collectives  46.2 us (21%)
  matrix products  34.6 us (16%)
  other arithmetic  19.7 us (9%)
  waiting for transfers between devices  18.7 us (9%)
  between operations  14.3 us (7%)
  starting transfers between devices  10.7 us (5%)
    gather x2, local copies, waits for them, and re-layouts, on_device(): natural_values = jnp.take_along_axis(basis, inverse[:, None, :], axis=2)  43 us
    dot_general x2, matrix products, near_block(): jnp.einsum('lkab,lksb->lsa', kernel_tiles, near_values, preferred_element...  24.3 us
    psum x1, blocking collectives, on_device(): new_norm = lax.psum(new_square, ('blk', 'leaf'))  21.7 us
    ppermute x2, waiting for transfers between devices, padded(): before = lax.ppermute(last, axis, up)  16.4 us
    all_gather x1, blocking collectives, on_device(): every_top = lax.all_gather(top_node[None], 'blk', axis=0, tiled=True)  13.5 us
    psum x1, blocking collectives, on_device(): top_node = lax.psum(lifted, 'leaf').astype(jnp.bfloat16)  11 us
    gather x2, local copies, waits for them, and re-layouts, near_block(): near_values = all_columns[slot_rows]  8.85 us
    ppermute x2, starting transfers between devices, padded(): after = lax.ppermute(initial, axis, down)  7.38 us
  transfers between devices with their start and end apart: 6, of which 2 were waited for; matrix products, arithmetic and copies ran while one was open for 52% of the time, Pallas kernels for 0%

commit v1 on v0

--- a/solution.py
+++ b/solution.py
@@ -151,7 +151,7 @@
     product_image = NUGGET * direction.astype(jnp.float32) + near_field + distant_field
     residual_next = residual - step[None, :, None] * product_image
     new_square = jnp.sum(residual_next * residual_next, axis=(0, 2))
-    new_norm = lax.psum(new_square, ("blk", "leaf"))
+    new_norm = lax.psum(lax.psum(new_square, "leaf"), "blk")
     beta_ratio = new_norm / old_norm
     direction_next = (
         residual_next + beta_ratio[None, :, None] * direction.astype(jnp.float32)

time: 218 us -> 227 us (1.041)
  blocking collectives: 46.2 us -> 55.2 us
    psum x1 -> x3, blocking collectives: 21.7 us -> 34.8 us  [the longest x1 21.1 us: on_device(): lax.psum(jnp.sum(residual * residual, axis=(0, 2)), ('blk', 'leaf'))]
    psum x1, blocking collectives: 11 us -> 7.08 us  [on_device(): top_node = lax.psum(lifted, 'leaf').astype(jnp.bfloat16)]
  transfers between devices with their start and end apart: 6 -> 6, of which waited for: 2 -> 2; matrix products, arithmetic and copies ran while one was open for 52% -> 50% of each run, Pallas kernels for 0% -> 0%
where the time goes in v1:
time: 227 us; the launch traced here: 226 us
  local copies, waits for them, and re-layouts  71.5 us (31%)
  blocking collectives  55.2 us (24%)
  matrix products  34.6 us (15%)
  other arithmetic  19.2 us (8%)
  waiting for transfers between devices  19.2 us (8%)
  between operations  14.2 us (6%)
  starting transfers between devices  10.7 us (5%)
    gather x2, local copies, waits for them, and re-layouts, on_device(): natural_values = jnp.take_along_axis(basis, inverse[:, None, :], axis=2)  43 us
    dot_general x2, matrix products, near_block(): jnp.einsum('lkab,lksb->lsa', kernel_tiles, near_values, preferred_element...  24.3 us
    psum x1, blocking collectives, on_device(): lax.psum(jnp.sum(residual * residual, axis=(0, 2)), ('blk', 'leaf'))  21.1 us
    ppermute x2, waiting for transfers between devices, padded(): before = lax.ppermute(last, axis, up)  16.8 us
    psum x2, blocking collectives, on_device(): new_norm = lax.psum(lax.psum(new_square, 'leaf'), 'blk')  13.7 us
    all_gather x1, blocking collectives, on_device(): every_top = lax.all_gather(top_node[None], 'blk', axis=0, tiled=True)  13.3 us
    gather x2, local copies, waits for them, and re-layouts, near_block(): near_values = all_columns[slot_rows]  8.86 us
    ppermute x2, starting transfers between devices, padded(): after = lax.ppermute(initial, axis, down)  7.76 us
  transfers between devices with their start and end apart: 6, of which 2 were waited for; matrix products, arithmetic and copies ran while one was open for 50% of the time, Pallas kernels for 0%

profile of v1, /device:TPU:0, one launch (start us, length us, event | category | flops | bytes accessed | tf_op | source)
XLA Modules:
  0.0 226.0 jit_solution(5271442602245252728)
XLA Ops:
  10.1 2.9 %collective-permute-start = (bf16[16,67,256]{2,0,1:T(8,128)(2,1)S(1)}, bf16[16,67,256]{2,0,1:T(8,128)(2,1)S(1)}, u32[]{:S(2)}, u32[]{:S(2)}) collective-permute-start(bf16[16,67,256]{2,0,1:T(8,128)(2,1)S(1)} %get-tuple-element.171), channel_id=1, source_target_pairs={{0,2},{2,4},{4,6},{6,8},{8,10},{10,12},{12,14},{14,0},{1,3},{3,5},... | collective-permute-start | bytes 1646600 | tf_op jit(solution)/shard_map/ppermute | solution.py:21
  13.1 3.0 %collective-permute-start.1 = (bf16[16,67,256]{2,0,1:T(8,128)(2,1)S(1)}, bf16[16,67,256]{2,0,1:T(8,128)(2,1)}, u32[]{:S(2)}, u32[]{:S(2)}) collective-permute-start(bf16[16,67,256]{2,0,1:T(8,128)(2,1)S(1)} %get-tuple-element.171), channel_id=1, source_target_pairs={{2,0},{4,2},{6,4},{8,6},{10,8},{12,10},{14,12},{0,14},{3,1},{5,3},... | collective-permute-start | bytes 1646600 | tf_op jit(solution)/shard_map/ppermute | solution.py:22
  19.7 16.8 %collective-permute-done = bf16[16,67,256]{2,0,1:T(8,128)(2,1)S(1)} collective-permute-done((bf16[16,67,256]{2,0,1:T(8,128)(2,1)S(1)}, bf16[16,67,256]{2,0,1:T(8,128)(2,1)S(1)}, u32[]{:S(2)}, u32[]{:S(2)}) %collective-permute-start) | collective-permute-done | bytes 548896 | tf_op jit(solution)/shard_map/ppermute | solution.py:21
  36.6 2.3 %collective-permute-done.1 = bf16[16,67,256]{2,0,1:T(8,128)(2,1)} collective-permute-done((bf16[16,67,256]{2,0,1:T(8,128)(2,1)S(1)}, bf16[16,67,256]{2,0,1:T(8,128)(2,1)}, u32[]{:S(2)}, u32[]{:S(2)}) %collective-permute-start.1) | collective-permute-done | bytes 548896 | tf_op jit(solution)/shard_map/ppermute | solution.py:22
  44.6 21.1 %psum.31 = f32[64]{0:T(128)} all-reduce(f32[64]{0:T(128)S(1)} %multiply_reduce_fusion), channel_id=1, replica_groups=mesh['groups'=2,'blk'=4,'leaf'=2,'sample'=2] {'blk','leaf'}, use_global_device_ids=true, to_apply=%region_8.9 | all-reduce | flops 64 | bytes 512 | tf_op jit(solution)/shard_map/psum | solution.py:70
  66.5 40.6 %gather_fusion.4 = bf16[4096,64]{1,0:T(8,128)(2,1)} fusion(bf16[16,64,256]{1,2,0:T(8,128)(2,1)S(1)} %copy.38, s32[4096]{0:T(1024)S(1)} %bitcast.104), kind=kCustom, calls=%fused_computation.4 | custom fusion | bytes 1081344 | tf_op jit(solution)/shard_map/jit(take_along_axis)/gather | solution.py:119
  107.0 2.4 %copy.39 = bf16[16,256,64]{1,2,0:T(8,128)(2,1)} copy(bf16[16,256,64]{2,1,0:T(8,128)(2,1)} %bitcast.109) | data formatting | bytes 1048576 | tf_op jit(solution)/shard_map/jit(take_along_axis)/gather | solution.py:119
  109.5 2.2 fusion.12
  111.7 4.7 %collective-permute-start.5 = (bf16[16,64,64]{1,2,0:T(8,128)(2,1)}, bf16[16,64,64]{1,2,0:T(8,128)(2,1)}, u32[]{:S(2)}, u32[]{:S(2)}) collective-permute-start(bf16[16,64,64]{1,2,0:T(8,128)(2,1)} %fusion.12), channel_id=1, source_target_pairs={{2,0},{4,2},{6,4},{8,6},{10,8},{12,10},{14,12},{0,14},{3,1},{5,3},... | collective-permute-start | bytes 393224 | tf_op jit(solution)/shard_map/ppermute | solution.py:22
  117.8 7.1 %psum.28 = bf16[64,64]{1,0:T(8,128)(2,1)S(1)} all-reduce(f32[64,64]{1,0:T(8,128)S(1)} %fusion.17), channel_id=1, replica_groups=mesh['groups'=2,'blk'=4,'leaf'=2,'sample'=2] {'leaf'}, use_global_device_ids=true, to_apply=%region_3.4 | all-reduce | flops 4096 | bytes 24576 | tf_op jit(solution)/shard_map/psum | solution.py:129
  124.8 13.3 %all-gather = bf16[256,64]{1,0:T(8,128)(2,1)S(1)} all-gather(bf16[64,64]{1,0:T(8,128)(2,1)S(1)} %psum.28), channel_id=2, replica_groups=mesh['groups'=2,'blk'=4,'leaf'=2,'sample'=2] {'blk'}, dimensions={0}, use_global_device_ids=true | all-gather | bytes 40960 | tf_op jit(solution)/shard_map/all_gather | solution.py:130
  141.4 3.1 %maximum_select_fusion = bf16[48,128,256]{2,0,1:T(8,128)(2,1)S(1)} fusion(bf16[48,64,256]{2,0,1:T(8,128)(2,1)} %collective-permute-done.2, bf16[48,64,256]{2,0,1:T(8,128)(2,1)} %slice.57, pred[]{:T(512)S(6)} %eq.12), kind=kLoop, calls=%fused_computation.28 | loop fusion | flops 4718592 | bytes 6291457 | tf_op jit(solution)/shard_map/jit(_where)/select_n | solution.py:81
  144.5 2.7 %copy.36 = bf16[48,128,256]{2,1,0:T(8,128)(2,1)} copy(bf16[48,128,256]{2,0,1:T(8,128)(2,1)S(1)} %maximum_select_fusion) | data formatting | bytes 6291456 | tf_op jit(solution)/shard_map/while | solution.py:108
  147.3 42.1 %while.12 = (s32[]{:T(128)}, f32[2,4,128,256]{3,2,1,0:T(8,128)}, s32[2]{0:T(128)S(1)}, s32[]{:T(128)}, s32[16,12]{1,0:T(8,128)}, /*index=5*/bf16[48,128,256]{2,1...) while((s32[]{:T(128)}, f32[2,4,128,256]{3,2,1,0:T(8,128)}, ...), condition=%wide.region_1.0_spmd, body=%wide.region_0.0_spmd.sunk | while | flops 852494208 | bytes 11184823 | solution.py:108
  151.0 4.4 %gather_fusion = bf16[48,128,256]{2,1,0:T(8,128)(2,1)} fusion(bf16[48,128,256]{2,1,0:T(8,128)(2,1)} %get-tuple-element.288, s32[1024]{0:T(1024)S(1)} %pad_clamp_fusion.4), kind=kCustom, calls=%fused_computation.clone.1 | custom fusion | bytes 6291648 | tf_op jit(solution)/shard_map/while/body/eval_jaxpr/gather | solution.py:95
  156.2 12.2 %fusion.54 = f32[2,4,128,256]{3,2,1,0:T(8,128)} fusion(f32[2,4,128,256]{3,2,1,0:T(8,128)} %get-tuple-element.268, s32[]{:T(128)} %get-tuple-element.267, bf16[4,12,128,256]{3,2,1,0:T(8,128)(2,1)} %bitcast.105, f32[4,12,256]{2,1,0:T(8,128)S(1)} %copy.62, f32[4,256]{1,0:T(4,128)S(1)} %get-tuple-element.246, f32[4,12,256]{2,1,0:T(8,128)S(1)} %copy.63, ...), kind=kOutput, calls=%fused_computation.8.clone.1 | convolution fusion | flops 852492288 | bytes 3830464 | tf_op jit(solution)/shard_map/while/body/eval_jaxpr/lkab,lksb->lsa/dot_general | solution.py:104
  172.1 4.4 %gather_fusion = bf16[48,128,256]{2,1,0:T(8,128)(2,1)} fusion(bf16[48,128,256]{2,1,0:T(8,128)(2,1)} %get-tuple-element.288, s32[1024]{0:T(1024)S(1)} %pad_clamp_fusion.4), kind=kCustom, calls=%fused_computation.clone.1 | custom fusion | bytes 6291648 | tf_op jit(solution)/shard_map/while/body/eval_jaxpr/gather | solution.py:95
  177.2 12.2 %fusion.54 = f32[2,4,128,256]{3,2,1,0:T(8,128)} fusion(f32[2,4,128,256]{3,2,1,0:T(8,128)} %get-tuple-element.268, s32[]{:T(128)} %get-tuple-element.267, bf16[4,12,128,256]{3,2,1,0:T(8,128)(2,1)} %bitcast.105, f32[4,12,256]{2,1,0:T(8,128)S(1)} %copy.62, f32[4,256]{1,0:T(4,128)S(1)} %get-tuple-element.246, f32[4,12,256]{2,1,0:T(8,128)S(1)} %copy.63, ...), kind=kOutput, calls=%fused_computation.8.clone.1 | convolution fusion | flops 852492288 | bytes 3830464 | tf_op jit(solution)/shard_map/while/body/eval_jaxpr/lkab,lksb->lsa/dot_general | solution.py:104
  193.5 2.2 gather_fusion.3
  195.7 1.9 constant_dynamic-slice_fusion
  198.6 4.6 %multiply_reduce_fusion.1 = (f32[64]{0:T(128)S(1)}, f32[16,64,256]{2,1,0:T(8,128)}) fusion(f32[16,64,256]{2,1,0:T(8,128)} %param.15, bf16[16,256,64]{1,2,0:T(8,128)(2,1)} %copy.39, pred[16,256]{1,0:T(8,128)(4,1)S(1)} %copy-done.12, f32[16,64,64]{2,1,0:T(8,128)} %convolution_bitcast_fusion.1, bf16[16,8,64,64]{2,3,1,0:T(8,128)(2,1)} %bitcast.107, ...), kind=kOutput, calls=%fused_computation.54 | convolution fusion | flops 103940032 | bytes 6558209 | tf_op jit(solution)/shard_map/bfw,baf->baw/dot_general | solution.py:148
  203.2 4.9 %psum.29 = f32[64]{0:T(128)S(1)} all-reduce(f32[64]{0:T(128)S(1)} %get-tuple-element.172), channel_id=1, replica_groups=mesh['groups'=2,'blk'=4,'leaf'=2,'sample'=2] {'leaf'}, use_global_device_ids=true, to_apply=%region_5.6 | all-reduce | flops 64 | bytes 512 | tf_op jit(solution)/shard_map/psum | solution.py:154
  208.1 8.8 %psum.30 = f32[64]{0:T(128)S(1)} all-reduce(f32[64]{0:T(128)S(1)} %psum.29), channel_id=1, replica_groups=mesh['groups'=2,'blk'=4,'leaf'=2,'sample'=2] {'blk'}, use_global_device_ids=true, to_apply=%region_6.7 | all-reduce | flops 64 | bytes 512 | tf_op jit(solution)/shard_map/psum | solution.py:154
  216.9 2.2 fusion.23
  (97 shorter events, 30.3 us)
Async XLA Ops:
  7.2 191.4 %copy-start = (bf16[16,8,64,64]{3,2,1,0:T(8,128)(2,1)S(1)}, bf16[16,8,64,64]{3,2,1,0:T(8,128)(2,1)}, u32[]{:S(2)}) copy-start(bf16[16,8,64,64]{3,2,1,0:T(8,128)(2,1)} %param.25) | copy-start | bytes 3145732
  7.2 58.5 %sort.19.cloned.1.call-start = ((), (), s32[]{:S(2)}) async-start(), calls=%async_computation | async-start | bytes 98336 | tf_op jit(solution)/shard_map/jit(argsort)/sort | solution.py:118
  10.1 31.1 %copy-start.1 = (bf16[16,67,256]{2,0,1:T(8,128)(2,1)}, bf16[16,67,256]{2,0,1:T(8,128)(2,1)S(1)}, u32[]{:S(2)}) copy-start(bf16[16,67,256]{2,0,1:T(8,128)(2,1)S(1)} %get-tuple-element.171) | copy-start | bytes 1646596
  10.1 26.4 %collective-permute-start = (bf16[16,67,256]{2,0,1:T(8,128)(2,1)S(1)}, bf16[16,67,256]{2,0,1:T(8,128)(2,1)S(1)}, u32[]{:S(2)}, u32[]{:S(2)}) collective-permute-start(bf16[16,67,256]{2,0,1:T(8,128)(2,1)S(1)} %get-tuple-element.171), channel_id=1, source_target_pairs={{0,2},{2,4},{4,6},{6,8},{8,10},{10,12},{12,14},{14,0},{1,3},{3,5},... | collective-permute-start | bytes 1646600 | tf_op jit(solution)/shard_map/ppermute | solution.py:21
  13.1 25.8 %collective-permute-start.1 = (bf16[16,67,256]{2,0,1:T(8,128)(2,1)S(1)}, bf16[16,67,256]{2,0,1:T(8,128)(2,1)}, u32[]{:S(2)}, u32[]{:S(2)}) collective-permute-start(bf16[16,67,256]{2,0,1:T(8,128)(2,1)S(1)} %get-tuple-element.171), channel_id=1, source_target_pairs={{2,0},{4,2},{6,4},{8,6},{10,8},{12,10},{14,12},{0,14},{3,1},{5,3},... | collective-permute-start | bytes 1646600 | tf_op jit(solution)/shard_map/ppermute | solution.py:22
  19.7 22.2 %copy-start.9 = (s32[16,12]{1,0:T(8,128)S(1)}, s32[16,12]{1,0:T(8,128)}, u32[]{:S(2)}) copy-start(s32[16,12]{1,0:T(8,128)} %param.23) | copy-start | bytes 2308
  36.6 4.7 %copy-start.4 = (bf16[16,67,256]{2,0,1:T(8,128)(2,1)}, bf16[16,67,256]{2,0,1:T(8,128)(2,1)S(1)}, u32[]{:S(2)}) copy-start(bf16[16,67,256]{2,0,1:T(8,128)(2,1)S(1)} %collective-permute-done) | copy-start | bytes 1646596
  41.3 100.2 %collective-permute-start.2 = (bf16[48,64,256]{2,0,1:T(8,128)(2,1)}, bf16[48,64,256]{2,0,1:T(8,128)(2,1)}, u32[]{:S(2)}, u32[]{:S(2)}) collective-permute-start(bf16[48,64,256]{2,0,1:T(8,128)(2,1)} %slice.57), channel_id=1, source_target_pairs={{0,1},{1,0},{2,3},{3,2},{4,5},{5,4},{6,7},{7,6},{8,9},{9,8},{10,11... | collective-permute-start | bytes 4718600 | tf_op jit(solution)/shard_map/ppermute | solution.py:28
  66.4 43.0 %copy-start.8 = (s32[16,256]{1,0:T(8,128)S(1)}, s32[16,256]{1,0:T(8,128)}, u32[]{:S(2)}) copy-start(s32[16,256]{1,0:T(8,128)} %get-tuple-element.131) | copy-start | bytes 49156
  66.5 50.0 %copy-start.7 = (bf16[1,64,64]{2,1,0:T(8,128)(2,1)S(1)}, bf16[1,64,64]{2,1,0:T(8,128)(2,1)}, u32[]{:S(2)}) copy-start(bf16[1,64,64]{2,1,0:T(8,128)(2,1)} %param.22) | copy-start | bytes 24580
  107.0 9.4 %copy-start.6 = (bf16[16,64,64]{2,1,0:T(8,128)(2,1)S(1)}, bf16[16,64,64]{2,1,0:T(8,128)(2,1)}, u32[]{:S(2)}) copy-start(bf16[16,64,64]{2,1,0:T(8,128)(2,1)} %param.21) | copy-start | bytes 393220
  107.0 33.6 %copy-start.2 = (bf16[16,67,256]{2,0,1:T(8,128)(2,1)S(1)}, bf16[16,67,256]{2,0,1:T(8,128)(2,1)}, u32[]{:S(2)}) copy-start(bf16[16,67,256]{2,0,1:T(8,128)(2,1)} %copy-done.1) | copy-start | bytes 1646596
  107.0 33.6 %copy-start.5 = (bf16[16,67,256]{2,0,1:T(8,128)(2,1)S(1)}, bf16[16,67,256]{2,0,1:T(8,128)(2,1)}, u32[]{:S(2)}) copy-start(bf16[16,67,256]{2,0,1:T(8,128)(2,1)} %copy-done.4) | copy-start | bytes 1646596
  109.5 2.2 copy-start.11
  111.7 80.5 %collective-permute-start.4 = (bf16[16,64,64]{1,2,0:T(8,128)(2,1)}, bf16[16,64,64]{1,2,0:T(8,128)(2,1)}, u32[]{:S(2)}, u32[]{:S(2)}) collective-permute-start(bf16[16,64,64]{1,2,0:T(8,128)(2,1)} %fusion.12), channel_id=1, source_target_pairs={{0,2},{2,4},{4,6},{6,8},{8,10},{10,12},{12,14},{14,0},{1,3},{3,5},... | collective-permute-start | bytes 393224 | tf_op jit(solution)/shard_map/ppermute | solution.py:21
  111.7 80.5 %collective-permute-start.5 = (bf16[16,64,64]{1,2,0:T(8,128)(2,1)}, bf16[16,64,64]{1,2,0:T(8,128)(2,1)}, u32[]{:S(2)}, u32[]{:S(2)}) collective-permute-start(bf16[16,64,64]{1,2,0:T(8,128)(2,1)} %fusion.12), channel_id=1, source_target_pairs={{2,0},{4,2},{6,4},{8,6},{10,8},{12,10},{14,12},{0,14},{3,1},{5,3},... | collective-permute-start | bytes 393224 | tf_op jit(solution)/shard_map/ppermute | solution.py:22
  147.3 46.2 %copy-start.10 = (s32[1024]{0:T(1024)S(1)}, s32[1024]{0:T(1024)}, u32[]{:S(2)}) copy-start(s32[1024]{0:T(1024)} %pad_clamp_fusion.1) | copy-start | bytes 12292
  191.2 6.4 %collective-permute-start.3 = (bf16[8,64,256]{2,1,0:T(8,128)(2,1)}, bf16[8,64,256]{2,1,0:T(8,128)(2,1)}, u32[]{:S(2)}, u32[]{:S(2)}) collective-permute-start(bf16[8,64,256]{2,1,0:T(8,128)(2,1)} %dynamic-slice_convert_fusion), channel_id=1, source_target_pairs={{0,1},{1,0},{2,3},{3,2},{4,5},{5,4},{6,7},{7,6},{8,9},{9,8},{10,11... | collective-permute-start | bytes 786440 | tf_op jit(solution)/shard_map/ppermute | solution.py:28
  193.5 5.1 %copy-start.3 = (bf16[16,64,256]{2,1,0:T(8,128)(2,1)S(1)}, bf16[16,64,256]{2,1,0:T(8,128)(2,1)}, u32[]{:S(2)}) copy-start(bf16[16,64,256]{2,1,0:T(8,128)(2,1)} %param.16) | copy-start | bytes 1572868
  193.5 5.1 %copy-start.12 = (pred[16,256]{1,0:T(8,128)(4,1)S(1)}, pred[16,256]{1,0:T(8,128)(4,1)}, u32[]{:S(2)}) copy-start(pred[16,256]{1,0:T(8,128)(4,1)} %copy-done.11) | copy-start | bytes 12292
  193.5 5.1 %copy-start.13 = (f32[64]{0:T(128)S(1)}, f32[64]{0:T(128)}, u32[]{:S(2)}) copy-start(f32[64]{0:T(128)} %param.17) | copy-start | bytes 772
  198.6 18.3 %copy-start.14 = (f32[64]{0:T(128)S(1)}, f32[64]{0:T(128)}, u32[]{:S(2)}) copy-start(f32[64]{0:T(128)} %psum.31) | copy-start | bytes 772
Sparse Core Ops, SparseCore 0:
  16.9 2.5 sort.21.cloned.1.call-done
  (1 shorter events, 0.0 us)
